TPU v7x, 32 devices: a whole 2x2x4 slice. The times are simulated.
32 devices in a mesh: img: 2 (over core), band: 4 (over z), pw: 4 (over y, x).
Axes of the slice: x: 2, y: 2, z: 4, core: 2. Of those that a mesh axis runs over, the one named last changes fastest.
Arguments:
- coefficients: bfloat16 [2, 1024, 32, 2048], P('img', None, ('band', 'pw')), may hold values from -6 to 6
- rotation: bfloat16 [2, 1024, 256], P('img'), may hold values from -0.1875 to 0.1875
- positions: int32 [2, 3, 256], P('img'), may hold values from 0 to 63, as said below
- start_pos: int32 [3, 256], replicated, may hold values from 0 to 63, as said below
- end_pos: int32 [3, 256], replicated, may hold values from 0 to 63, as said below
- species: int32 [256], replicated, may hold values from 0 to 3
- depth: float32 [4], replicated, may hold values from 0.5 to 3
Outputs:
- correction: bfloat16 [2, 256, 32, 2048], P('img', None, ('band', 'pw'))
- ritz_values: float32 [2, 256], P('img')
- band_force: float32 [2, 3, 256], P('img')
- along_force: float32 [2], P('img')
Inputs may be any that keep to these rules, and one draw needn't show every extreme that they name: `positions`: grid index of each atom's centre along each dimension. `start_pos`: grid index of each atom's centre along each dimension. `end_pos`: grid index of each atom's centre along each dimension.
All inputs are finite; a program needn't handle non-finite values.
Results may differ from a plain program's by a relative error of at most 0.012.
The roundings to bfloat16 on the way count: a program that leaves them out, or rounds other values in their place, can miss the bound.
Values may be sent and summed in bfloat16 or wider, within the bound.
A program may use at most 128 MiB of HBM per device.

v0:
```python
import math
import jax
import jax.numpy as jnp
from jax import lax
from jax.sharding import PartitionSpec as P

G = 64
W = 32
BANDS = 1024
BLOCK = 256
SPECIES = 4
kinetic_scale = 0.01
sigma_cells = 3.0
spring_constant = 2.0
epsilon = 1e-06
highest = lax.Precision.HIGHEST


def passed_along(block, axis, distance):
    devices = range(lax.axis_size(axis))
    route = [(i - distance, i) for i in devices if i - distance in devices]
    return lax.ppermute(block, axis, route)


def phases(box_order, box_size, grid_size):
    wavenum = box_order - box_size // 2
    grid_cells = jnp.arange(grid_size, dtype=jnp.int32)
    turn_count = jnp.mod(wavenum[:, None] * grid_cells[None, :], grid_size)
    return turn_count.astype(jnp.float32) * (2.0 * math.pi / grid_size)


def forward_table(box_order, box_size, grid_size):
    angle_tab = phases(box_order, box_size, grid_size)
    cosine = jnp.cos(angle_tab) / math.sqrt(box_size)
    sine_part = jnp.sin(angle_tab) / math.sqrt(box_size)
    dft_table = jnp.stack(
        [jnp.stack([cosine, sine_part], 1), jnp.stack([-sine_part, cosine], 1)], 0
    )
    return dft_table.astype(jnp.bfloat16)


def inverse_table(box_order, box_size, grid_size):
    angle_tab = phases(box_order, box_size, grid_size).T
    factor = math.sqrt(box_size) / grid_size
    cosine = jnp.cos(angle_tab) * factor
    sine_part = jnp.sin(angle_tab) * factor
    dft_table = jnp.stack(
        [jnp.stack([cosine, -sine_part], 1), jnp.stack([sine_part, cosine], 1)], 0
    )
    return dft_table.astype(jnp.bfloat16)


def section_zy(coeff_block, table_z, table_y):
    leading = coeff_block.shape[0]
    planes = coeff_block.shape[1]
    split_up = coeff_block.reshape(leading, planes, W, 2, W)
    along_z = jnp.einsum(
        "blyck,ckdn->blydn", split_up, table_z, preferred_element_type=jnp.float32
    ).astype(jnp.bfloat16)
    along_y = jnp.einsum(
        "blycz,cydm->blmdz", along_z, table_y, preferred_element_type=jnp.float32
    ).astype(jnp.bfloat16)
    return along_y.reshape(leading, planes, G * 2 * G)


def section_x(arrived, table_x):
    leading = arrived.shape[0]
    y_rows = arrived.shape[2] // (2 * G)
    split_up = arrived.reshape(leading, W, y_rows, 2, G)
    return jnp.einsum("bxycz,cxdn->bnydz", split_up, table_x, preferred_element_type=jnp.float32)


def section_x_inverse(weighted, table_x):
    leading = weighted.shape[0]
    y_rows = weighted.shape[2]
    along_x = jnp.einsum(
        "bnydz,dncx->bxycz", weighted, table_x, preferred_element_type=jnp.float32
    ).astype(jnp.bfloat16)
    return along_x.reshape(leading, W, y_rows * 2 * G)


def section_zy_inverse(returned, table_y, table_z):
    leading = returned.shape[0]
    planes = returned.shape[1]
    split_up = returned.reshape(leading, planes, G, 2, G)
    along_y = jnp.einsum(
        "blmdz,dmcy->blycz", split_up, table_y, preferred_element_type=jnp.float32
    ).astype(jnp.bfloat16)
    along_z = jnp.einsum("blydn,dnck->blyck", along_y, table_z, preferred_element_type=jnp.float32)
    return along_z.reshape(leading, planes, W * 2 * W)


def wrap_offset(values):
    return jnp.mod(values + G // 2, G) - G // 2


def gaussians(coords, grid_cells):
    offset = wrap_offset(grid_cells[None, :] - coords[:, None]).astype(jnp.float32)
    return (jnp.exp(-offset * offset / (2.0 * sigma_cells * sigma_cells)), offset)


def atom_tables(own_pos, y_cells):
    grid_cells = jnp.arange(G, dtype=jnp.int32)
    gauss_x, offset_x = gaussians(own_pos[0], grid_cells)
    gauss_y, offset_y = gaussians(own_pos[1], y_cells)
    gauss_z, offset_z = gaussians(own_pos[2], grid_cells)
    return (gauss_x, offset_x, gauss_y, offset_y, gauss_z, offset_z)


def local_potential(tables, strength):
    gauss_x, offset_x, gauss_y, offset_y, gauss_z, offset_z = tables
    atom_count = gauss_x.shape[0]
    joined = (gauss_y[:, :, None] * gauss_z[:, None, :]).reshape(atom_count, -1)
    potential = jnp.dot((strength[:, None] * gauss_x).T, joined, precision=highest)
    return (potential, joined)


def atom_forces(density, tables, joined, strength):
    gauss_x, offset_x, gauss_y, offset_y, gauss_z, offset_z = tables
    atom_count = gauss_x.shape[0]
    with_y = ((gauss_y * offset_y)[:, :, None] * gauss_z[:, None, :]).reshape(atom_count, -1)
    with_z = (gauss_y[:, :, None] * (gauss_z * offset_z)[:, None, :]).reshape(atom_count, -1)
    stacked = jnp.concatenate([joined, with_y, with_z], 0)
    moments = jnp.dot(density, stacked.T, precision=highest)
    prefactor = -strength / (sigma_cells * sigma_cells)
    force_x = prefactor * jnp.sum(gauss_x * offset_x * moments[:, :atom_count].T, 1)
    force_y = prefactor * jnp.sum(gauss_x * moments[:, atom_count : 2 * atom_count].T, 1)
    force_z = prefactor * jnp.sum(gauss_x * moments[:, 2 * atom_count :].T, 1)
    return jnp.stack([force_x, force_y, force_z], 0)


def space_work(in_space, own_pos, strength, y_rows):
    y_cells = jnp.arange(y_rows, dtype=jnp.int32)
    tables = atom_tables(own_pos, y_cells)
    potential, joined = local_potential(tables, strength)
    grid_potential = potential.reshape(G, y_rows, G)
    density = jnp.sum(in_space * in_space, axis=(0, 3)).reshape(G, y_rows * G) / BLOCK
    force_part = atom_forces(density, tables, joined, strength)
    weighted = (in_space * grid_potential[:, :, None, :]).astype(jnp.bfloat16)
    return (weighted, force_part)


def kinetic_table(x_cells):
    entries = jnp.arange(W * 2 * W, dtype=jnp.int32)
    wave_y = entries // (2 * W) - W // 2
    wave_z = jnp.mod(entries, W) - W // 2
    wave_x = x_cells - W // 2
    squared = wave_x[:, None] * wave_x[:, None] + (wave_y * wave_y + wave_z * wave_z)[None, :]
    return kinetic_scale * 0.5 * squared.astype(jnp.float32)


def rotate_quarter(values):
    leading = values.shape[0]
    middle = values.shape[1]
    split_up = values.reshape(leading, middle, W, 2, W)
    turned = jnp.stack([-split_up[:, :, :, 1, :], split_up[:, :, :, 0, :]], 3)
    return turned.reshape(values.shape)


def chain_forces(force, own_pos, before, after):
    ahead_step = wrap_offset(after - own_pos).astype(jnp.float32)
    behind = wrap_offset(own_pos - before).astype(jnp.float32)
    tangent_raw = ahead_step + behind
    entries = 3 * own_pos.shape[1]
    tangent = (
        tangent_raw * lax.rsqrt(jnp.mean(tangent_raw * tangent_raw) + epsilon) / math.sqrt(entries)
    )
    length_ahead = jnp.sqrt(entries * (jnp.mean(ahead_step * ahead_step) + epsilon))
    length_behind = jnp.sqrt(entries * (jnp.mean(behind * behind) + epsilon))
    along_path = jnp.sum(force * tangent)
    band_push = (
        force - along_path * tangent + spring_constant * (length_ahead - length_behind) * tangent
    )
    return (band_push, along_path)


def body(coefficients, rotation, positions, start_pos, end_pos, species, depth):
    coeff_all = coefficients[0]
    planes = coeff_all.shape[1]
    flat_all = coeff_all.reshape(BANDS, -1)
    orbitals = jnp.einsum("ib,ik->bk", rotation[0], flat_all, preferred_element_type=jnp.float32)
    orbitals = orbitals.astype(jnp.bfloat16).reshape(BLOCK, planes, W * 2 * W)
    kind_ids = jnp.arange(SPECIES, dtype=jnp.int32)
    strength = jnp.sum(jnp.where(species[:, None] == kind_ids[None, :], depth[None, :], 0.0), 1)
    own_pos = positions[0]
    natural = jnp.arange(W, dtype=jnp.int32)
    table_f = forward_table(natural, W, G)
    table_i = inverse_table(natural, W, G)
    whole_vectors = lax.all_to_all(
        orbitals, ("band", "pw"), split_axis=0, concat_axis=1, tiled=True
    )
    spread = section_zy(whole_vectors, table_f, table_f)
    weighted, force_part = space_work(section_x(spread, table_f), own_pos, strength, G)
    partial_apply = section_zy_inverse(section_x_inverse(weighted, table_i), table_i, table_i)
    applied = lax.all_to_all(partial_apply, ("band", "pw"), split_axis=1, concat_axis=0, tiled=True)
    x_cells = lax.axis_index(("band", "pw")) * planes + jnp.arange(planes, dtype=jnp.int32)
    kinetic = kinetic_table(x_cells)
    orbitals_wide = orbitals.astype(jnp.float32)
    hamiltonian = kinetic[None] * orbitals_wide + applied
    numerator = jnp.sum(orbitals_wide * hamiltonian, axis=(1, 2))
    denominator = jnp.sum(orbitals_wide * orbitals_wide, axis=(1, 2))
    numerator, denominator, atom_force = lax.psum(
        (numerator, denominator, force_part), ("band", "pw")
    )
    npw_total = W * W * W
    ritz_values = numerator / npw_total / (denominator / npw_total + epsilon)
    residual = hamiltonian - ritz_values[:, None, None] * orbitals_wide
    search = (residual / (1.0 + kinetic)[None]).astype(jnp.bfloat16)
    search_pair = jnp.concatenate(
        [search.reshape(BLOCK, -1), (-rotate_quarter(search)).reshape(BLOCK, -1)], 0
    )
    intersections = (
        jnp.einsum("ik,jk->ij", flat_all, search_pair, preferred_element_type=jnp.float32)
        / npw_total
    )
    intersections = lax.psum(intersections, ("band", "pw")).astype(jnp.bfloat16)
    projected = jnp.einsum("ij,ik->jk", intersections, flat_all, preferred_element_type=jnp.float32)
    projection = projected[:BLOCK].reshape(BLOCK, planes, -1) + rotate_quarter(
        projected[BLOCK:].reshape(BLOCK, planes, -1)
    )
    correction = (search.astype(jnp.float32) - projection).astype(jnp.bfloat16)
    image_idx = lax.axis_index("img")
    before = passed_along(own_pos, "img", 1)
    after = passed_along(own_pos, "img", -1)
    before = jnp.where(image_idx == 0, start_pos, before)
    after = jnp.where(image_idx == lax.axis_size("img") - 1, end_pos, after)
    band_push, along_path = chain_forces(atom_force, own_pos, before, after)
    return (correction[None], ritz_values[None], band_push[None], along_path[None])


def solution(mesh):
    in_specs = (
        P("img", None, ("band", "pw"), None),
        P("img", None, None),
        P("img", None, None),
        P(),
        P(),
        P(),
        P(),
    )
    out_specs = (
        P("img", None, ("band", "pw"), None),
        P("img", None),
        P("img", None, None),
        P("img"),
    )
    return jax.shard_map(body, mesh=mesh, in_specs=in_specs, out_specs=out_specs, check_vma=False)
```

profile of v0, /device:TPU:0, one launch (start us, length us, event | category | flops | bytes accessed | tf_op | source)
XLA Modules:
  0.0 592.1 jit_solution(8768601264481166253)
XLA Ops:
  0.6 12.1 %copy.141 = bf16[128,8,2,2048]{3,1,2,0:T(8,128)(2,1)} copy(bf16[128,8,2,2048]{3,2,1,0:T(2,128)(2,1)} %bitcast.208) | data formatting | bytes 16777216
  12.7 5.8 convolution_convert_fusion
  18.5 2.8 reshape.676
  21.3 8.6 %all-to-all-start = ((bf16[256,2,2048]{2,1,0:T(2,128)(2,1)}), bf16[256,2,2048]{2,1,0:T(2,128)(2,1)}, u32[]{:S(2)}, u32[]{:S(2)}) async-start(bf16[256,2,2048]{2,1,0:T(2,128)(2,1)} %reshape.676), calls=%async_computation | async-start | bytes 4194304 | tf_op jit(solution)/shard_map/all_to_all | solution.py:189
  30.5 7.5 %fusion.29 = f32[64,64,64]{2,0,1:T(8,128)} fusion(f32[256,64]{0,1:T(8,128)S(1)} %get-tuple-element.67, f32[256,64]{0,1:T(8,128)S(1)} %get-tuple-element.74, s32[256]{0:T(256)S(1)} %bitcast.217, f32[256]{0:T(256)S(1)} %select_reduce_fusion), kind=kOutput, calls=%fused_computation.35 | convolution fusion | flops 806666240 | bytes 1181696 | tf_op jit(solution)/shard_map/dot_general | solution.py:114
  37.9 35.0 %all-to-all-done = bf16[256,2,2048]{2,1,0:T(2,128)(2,1)} async-done(((bf16[256,2,2048]{2,1,0:T(2,128)(2,1)}), bf16[256,2,2048]{2,1,0:T(2,128)(2,1)}, u32[]{:S(2)}, u32[]{:S(2)}) %all-to-all-start) | async-done | bytes 2097184 | tf_op jit(solution)/shard_map/all_to_all | solution.py:189
  72.9 2.5 copy.101
  75.4 1.5 copy.102
  76.9 17.9 %reshape.677 = bf16[16,32,32,2,32]{4,3,2,0,1:T(2,128)(2,1)} reshape(bf16[16,16,2,2048]{3,0,2,1:T(8,128)(2,1)} %copy.102) | data formatting | bytes 4194304 | tf_op jit(solution)/shard_map/reshape | solution.py:56
  94.8 12.6 %fusion.20 = bf16[16,32,64,2,64]{4,2,1,0,3:T(8,128)(2,1)} fusion(bf16[16,32,32,2,32,1]{4,3,2,0,1,5:T(2,128)(2,1)} %bitcast.203, bf16[1,32,2,64]{3,1,0,2:T(8,128)(2,1)S(1)} %get-tuple-element.57, bf16[1,32,2,64]{3,1,0,2:T(8,128)(2,1)S(1)} %get-tuple-element.56), kind=kOutput, calls=%fused_computation.24 | convolution fusion | flops 811663360 | bytes 10502144 | tf_op jit(solution)/shard_map/blycz,cydm->blmdz/dot_general | solution.py:60
  107.4 28.7 %fusion.1 = (f32[64,64,64]{2,0,1:T(8,128)}, bf16[16,64,64,2,64]{4,1,2,0,3:T(8,128)(2,1)}) fusion(f32[64,64,64]{2,0,1:T(8,128)} %fusion.29, bf16[16,32,64,2,64]{4,2,1,0,3:T(8,128)(2,1)} %fusion.20, bf16[1,32,2,64]{3,1,0,2:T(8,128)(2,1)S(1)} %get-tuple-element.57, bf16[1,32,2,64]{3,1,0,2:T(8,128)(2,1)S(1)} %get-tuple-element.56), kind=kOutput, calls=%fused_computation.3 | convolution fusion | flops 1107066880 | bytes 27279360 | tf_op jit(solution)/shard_map/bxycz,cxdn->bnydz/dot_general | solution.py:70
  136.1 18.9 %fusion.6 = bf16[16,32,64,2,64,1]{4,1,2,0,3,5:T(8,128)(2,1)} fusion(bf16[16,64,64,2,64]{4,1,2,0,3:T(8,128)(2,1)} %get-tuple-element.40, bf16[1,64,2,32]{1,3,0,2:T(8,128)(2,1)S(1)} %get-tuple-element.55, bf16[1,64,2,32]{1,3,0,2:T(8,128)(2,1)S(1)} %get-tuple-element.54), kind=kOutput, calls=%fused_computation.10 | convolution fusion | flops 1077968896 | bytes 25182208 | tf_op jit(solution)/shard_map/bnydz,dncx->bxycz/dot_general | solution.py:76
  155.0 19.3 %convolution_bitcast_fusion = f32[16,32,32,2,32]{4,2,3,1,0:T(8,128)} fusion(bf16[16,32,64,2,64,1]{4,1,2,0,3,5:T(8,128)(2,1)} %fusion.6, bf16[1,64,2,32]{1,3,0,2:T(8,128)(2,1)S(1)} %get-tuple-element.55, bf16[1,64,2,32]{1,3,0,2:T(8,128)(2,1)S(1)} %get-tuple-element.54), kind=kOutput, calls=%fused_computation.25 | convolution fusion | flops 807469056 | bytes 12599296 | tf_op jit(solution)/shard_map/blydn,dnck->blyck/dot_general | solution.py:89
  174.3 28.6 %copy.138 = f32[16,32,32,2,32]{4,3,2,0,1:T(2,128)} copy(f32[16,32,32,2,32]{4,2,3,1,0:T(8,128)} %convolution_bitcast_fusion) | data formatting | bytes 8388608 | tf_op jit(solution)/shard_map/reshape | solution.py:90
  202.9 21.7 %reshape.699 = f32[16,32,2048]{2,0,1:T(8,128)} reshape(f32[16,32,32,2,32]{4,3,2,0,1:T(2,128)} %copy.138) | data formatting | bytes 8388608 | tf_op jit(solution)/shard_map/reshape | solution.py:90
  224.6 10.1 %all-to-all-start.1 = ((f32[16,32,2048]{2,0,1:T(8,128)}), f32[16,32,2048]{2,0,1:T(8,128)}, u32[]{:S(2)}, u32[]{:S(2)}) async-start(f32[16,32,2048]{2,0,1:T(8,128)} %reshape.699), calls=%async_computation.1 | async-start | bytes 8388608 | tf_op jit(solution)/shard_map/all_to_all | solution.py:195
  234.7 1.3 collective-permute-start
  236.0 3.0 collective-permute-start.1
  239.4 5.0 broadcast_multiply_fusion.2
  244.5 3.0 copy.112
  247.5 5.1 reshape.682
  256.0 1.8 broadcast_multiply_fusion.4
  257.8 2.5 copy.119
  260.3 3.1 div.129
  263.4 12.6 %fusion.14 = f32[64,768]{1,0:T(8,128)S(1)} fusion(f32[64,4096]{1,0:T(8,128)} %div.129, f32[256,4096]{0,1:T(8,128)} %bitcast.212, f32[256,4096]{0,1:T(8,128)} %bitcast.213, f32[256,4096]{0,1:T(8,128)} %bitcast.211), kind=kOutput, calls=%fused_computation.18 | convolution fusion | flops 2422210560 | bytes 13828096 | tf_op jit(solution)/shard_map/dot_general | solution.py:124
  276.2 36.9 %all-to-all-done.1 = f32[16,32,2048]{2,0,1:T(8,128)} async-done(((f32[16,32,2048]{2,0,1:T(8,128)}), f32[16,32,2048]{2,0,1:T(8,128)}, u32[]{:S(2)}, u32[]{:S(2)}) %all-to-all-start.1) | async-done | bytes 4194336 | tf_op jit(solution)/shard_map/all_to_all | solution.py:195
  313.0 5.5 copy.110
  318.5 4.7 copy.109
  323.2 5.9 %copy.143 = f32[32,8,2,2048]{3,1,2,0:T(8,128)} copy(f32[32,8,2,2048]{3,2,1,0:T(2,128)S(1)} %bitcast.206) | data formatting | bytes 8388608
  329.1 18.0 %all_to_all.36 = f32[256,2,32,2,32]{4,3,2,0,1:T(2,128)} reshape(f32[16,16,2,2048]{3,1,0,2:T(8,128)} %copy.109) | data formatting | bytes 8388608 | tf_op jit(solution)/shard_map/all_to_all | solution.py:195
  347.1 20.8 %copy.114 = f32[256,2,32,2,32]{0,4,3,2,1:T(8,128)} copy(f32[256,2,32,2,32]{4,3,2,0,1:T(2,128)} %all_to_all.36) | data formatting | bytes 8388608 | tf_op jit(solution)/shard_map/all_to_all | solution.py:195
  367.9 3.3 fusion.37
  371.1 54.3 %all-reduce.1 = (f32[256]{0:T(256)S(1)}, f32[256]{0:T(256)S(1)}) all-reduce(f32[256]{0:T(256)S(1)} %get-tuple-element.25, f32[256]{0:T(256)S(1)} %get-tuple-element.24), channel_id=1, replica_groups=mesh['img'=2,'band'=4,'pw'=4] {'band','pw'}, use_global_device_ids=true, to_apply=%region_4.5 | all-reduce | flops 512 | bytes 4096 | tf_op jit(solution)/shard_map/psum | solution.py:202
  425.5 4.6 fusion.41
  430.2 0.8 copy-done.3
  431.0 1.5 divide_convert_fusion
  432.8 2.9 copy.115
  435.7 8.2 %multiply_bitcast_fusion = f32[1024,512]{0,1:T(8,128)S(1)} fusion(bf16[1024,4096]{1,0:T(8,128)(2,1)} %bitcast.199, bf16[256,4096]{1,0:T(8,128)(2,1)} %copy.115, bf16[256,4096]{1,0:T(8,128)(2,1)} %fusion.41), kind=kOutput, calls=%fused_computation.59 | convolution fusion | flops 4303880192 | bytes 14680064 | tf_op jit(solution)/shard_map/ik,jk->ij/dot_general | solution.py:213
  444.0 97.9 %all-reduce.3 = (bf16[1024,512]{0,1:T(8,128)(2,1)}, f32[3,256]{1,0:T(4,128)S(1)}) all-reduce(f32[1024,512]{0,1:T(8,128)S(1)} %multiply_bitcast_fusion, f32[3,256]{1,0:T(4,128)S(1)} %pad_maximum_fusion.9), channel_id=1, replica_groups=mesh['img'=2,'band'=4,'pw'=4] {'band','pw'}, use_global_device_ids=true, to_apply=%region_5.6 | all-reduce | flops 525056 | bytes 3151872 | tf_op jit(solution)/shard_map/psum | solution.py:216
  543.7 7.2 %fusion.152 = f32[512,4096]{1,0:T(8,128)S(1)} fusion(bf16[1024,512]{0,1:T(8,128)(2,1)} %get-tuple-element.29, bf16[1024,4096]{1,0:T(8,128)(2,1)} %bitcast.200), kind=kOutput, calls=%fused_computation.217 | convolution fusion | flops 4294967296 | bytes 17825792 | tf_op jit(solution)/shard_map/ij,ik->jk/dot_general | solution.py:217
  550.9 3.8 fusion.146
  554.6 5.6 copy.116
  560.2 2.8 slice_negate_fusion
  563.0 2.4 pad_maximum_fusion
  565.5 5.4 copy.118
  570.9 6.6 %reshape.680 = f32[1,256,2,2048]{3,2,1,0:T(2,128)} reshape(f32[256,4096]{1,0:T(8,128)} %get-tuple-element.41) | data formatting | bytes 8388608 | tf_op jit(solution)/shard_map/reshape | solution.py:218
  577.4 10.7 %fusion.35 = bf16[1,256,2,2048]{3,1,2,0:T(8,128)(2,1)S(1)} fusion(f32[1,256,2,2048]{3,1,2,0:T(8,128)} %copy.118, f32[1,256,2,2048]{3,2,1,0:T(2,128)} %reshape.680, f32[16,16,2,2048]{3,1,0,2:T(8,128)} %copy.109, f32[1,256,2,2048]{3,2,1,0:T(2,128)} %reshape.682, f32[2,2048]{1,0:T(2,128)S(1)} %get-tuple-element.53, f32[256]{0:T(256)S(1)} %add_divide_fusion, ...), kind=kLoop, calls=%fused_computation.43 | loop fusion | flops 10485760 | bytes 18908160 | tf_op jit(solution)/shard_map/convert_element_type | solution.py:221
  588.1 3.5 copy.120
  (50 shorter events, 3.9 us)
Async XLA Ops:
  0.6 12.1 %copy-start = (bf16[1,1024,256]{2,1,0:T(8,128)(2,1)S(1)}, bf16[1,1024,256]{2,1,0:T(8,128)(2,1)}, u32[]{:S(2)}) copy-start(bf16[1,1024,256]{2,1,0:T(8,128)(2,1)} %param.8) | copy-start | bytes 1572868
  18.5 11.8 %copy-start.8 = (s32[256]{0:T(256)S(1)}, s32[256]{0:T(256)}, u32[]{:S(2)}) copy-start(s32[256]{0:T(256)} %param.12) | copy-start | bytes 3076
  18.5 11.8 %copy-start.9 = (f32[4]{0:T(128)S(1)}, f32[4]{0:T(128)}, u32[]{:S(2)}) copy-start(f32[4]{0:T(128)} %param.13) | copy-start | bytes 52
  18.5 11.9 %copy-start.4 = (s32[1,3,256]{2,0,1:T(1,128)S(1)}, s32[1,3,256]{2,0,1:T(1,128)}, u32[]{:S(2)}) copy-start(s32[1,3,256]{2,0,1:T(1,128)} %param.9) | copy-start | bytes 9220
  21.3 51.6 %all-to-all-start = ((bf16[256,2,2048]{2,1,0:T(2,128)(2,1)}), bf16[256,2,2048]{2,1,0:T(2,128)(2,1)}, u32[]{:S(2)}, u32[]{:S(2)}) async-start(bf16[256,2,2048]{2,1,0:T(2,128)(2,1)} %reshape.676), calls=%async_computation | async-start | bytes 4194304 | tf_op jit(solution)/shard_map/all_to_all | solution.py:189
  224.6 88.5 %all-to-all-start.1 = ((f32[16,32,2048]{2,0,1:T(8,128)}), f32[16,32,2048]{2,0,1:T(8,128)}, u32[]{:S(2)}, u32[]{:S(2)}) async-start(f32[16,32,2048]{2,0,1:T(8,128)} %reshape.699), calls=%async_computation.1 | async-start | bytes 8388608 | tf_op jit(solution)/shard_map/all_to_all | solution.py:195
  234.7 18.0 %collective-permute-start = (s32[3,256]{1,0:T(4,128)S(1)}, s32[3,256]{1,0:T(4,128)S(1)}, u32[]{:S(2)}, u32[]{:S(2)}) collective-permute-start(s32[3,256]{1,0:T(4,128)S(1)} %bitcast.224), channel_id=1, source_target_pairs={{16,0},{17,1},{18,2},{19,3},{20,4},{21,5},{22,6},{23,7},{24,8},{25... | collective-permute-start | bytes 9224 | tf_op jit(solution)/shard_map/ppermute | solution.py:22
  236.0 16.7 %collective-permute-start.1 = (s32[3,256]{1,0:T(4,128)S(1)}, s32[3,256]{1,0:T(4,128)S(1)}, u32[]{:S(2)}, u32[]{:S(2)}) collective-permute-start(s32[3,256]{1,0:T(4,128)S(1)} %bitcast.225), channel_id=1, source_target_pairs={{0,16},{1,17},{2,18},{3,19},{4,20},{5,21},{6,22},{7,23},{8,24},{9,... | collective-permute-start | bytes 9224 | tf_op jit(solution)/shard_map/ppermute | solution.py:22
  247.5 5.2 copy-start.6
  247.5 5.2 copy-start.7
  425.5 151.9 %copy-start.5 = (f32[256]{0:T(256)}, f32[256]{0:T(256)S(1)}, u32[]{:S(2)}) copy-start(f32[256]{0:T(256)S(1)} %add_divide_fusion) | copy-start | bytes 3076
  425.5 4.7 copy-start.2
  425.5 5.5 copy-start.3
  577.4 14.2 %copy-start.1 = (bf16[1,1024,256]{2,1,0:T(8,128)(2,1)S(1)}, bf16[1,1024,256]{2,1,0:T(8,128)(2,1)}, u32[]{:S(2)}) copy-start(bf16[1,1024,256]{2,1,0:T(8,128)(2,1)} %param.8) | copy-start | bytes 1572868
where the time goes:
time: 600 us; the launch traced here: 592 us
  local copies, waits for them, and re-layouts  185 us (31%)
  blocking collectives  152 us (25%)
  matrix products  121 us (20%)
  waiting for transfers between devices  71.8 us (12%)
  other arithmetic  35.2 us (6%)
  starting transfers between devices  23 us (4%)
    psum x1, blocking collectives, body(): intersections = lax.psum(intersections, ('band', 'pw')).astype(jnp.bfloat16)  97.9 us
    psum x1, blocking collectives, body(): lax.psum((numerator, denominator, force_part), ('band', 'pw'))  54.3 us
    reshape x2, local copies, waits for them, and re-layouts, section_zy_inverse(): return along_z.reshape(leading, planes, W * 2 * W)  50.3 us
    all_to_all x4, local copies, waits for them, and re-layouts, body(): lax.all_to_all(partial_apply, ('band', 'pw'), split_axis=1, concat_axis=0...  48.9 us
    all_to_all x1, waiting for transfers between devices, body(): lax.all_to_all(partial_apply, ('band', 'pw'), split_axis=1, concat_axis=0...  36.9 us
    all_to_all x1, waiting for transfers between devices, body(): lax.all_to_all(orbitals, ('band', 'pw'), split_axis=0, concat_axis=1, til...  35 us
    dot_general x1, matrix products, section_x(): jnp.einsum('bxycz,cxdn->bnydz', split_up, table_x, preferred_element_type...  28.7 us
    unnamed x26, local copies, waits for them, and re-layouts  22.4 us
  transfers between devices with their start and end apart: 4, of which 2 were waited for; matrix products, arithmetic and copies ran while one was open for 7% of the time, Pallas kernels for 0%

commit v1 on v0

--- a/solution.py
+++ b/solution.py
@@ -192,7 +192,9 @@
     spread = section_zy(whole_vectors, table_f, table_f)
     weighted, force_part = space_work(section_x(spread, table_f), own_pos, strength, G)
     partial_apply = section_zy_inverse(section_x_inverse(weighted, table_i), table_i, table_i)
-    applied = lax.all_to_all(partial_apply, ("band", "pw"), split_axis=1, concat_axis=0, tiled=True)
+    pieces = jnp.split(partial_apply, lax.axis_size(("band", "pw")), axis=1)
+    received = lax.all_to_all(jnp.stack(pieces), ("band", "pw"), 0, 0)
+    applied = jnp.concatenate(received, axis=0)
     x_cells = lax.axis_index(("band", "pw")) * planes + jnp.arange(planes, dtype=jnp.int32)
     kinetic = kinetic_table(x_cells)
     orbitals_wide = orbitals.astype(jnp.float32)

time: 600 us -> 639 us (1.065)
  local copies, waits for them, and re-layouts: 185 us -> 209 us
  matrix products: 121 us -> 136 us
    all_to_all x4 -> x0, local copies, waits for them, and re-layouts: 48.9 us -> none  [body(): lax.all_to_all(partial_apply, ('band', 'pw'), split_axis=1, concat_axis=0...]
    reshape x1 -> x3, local copies, waits for them, and re-layouts: 5.4 us -> 46.9 us  [body(): applied = jnp.concatenate(received, axis=0)]
    unnamed x26 -> x45, local copies, waits for them, and re-layouts: 22.4 us -> 57.7 us
    reshape x2 -> x1, local copies, waits for them, and re-layouts: 50.3 us -> 21.7 us  [section_zy_inverse(): return along_z.reshape(leading, planes, W * 2 * W)]
    dot_general x0 -> x1, local copies, waits for them, and re-layouts: none -> 28.5 us  [section_zy_inverse(): jnp.einsum('blydn,dnck->blyck', along_y, table_z, preferred_element_type=...]
    dot_general x1, matrix products: 28.7 us -> 43.8 us  [section_x(): jnp.einsum('bxycz,cxdn->bnydz', split_up, table_x, preferred_element_type...]
    convert_element_type x1, other arithmetic: 10.7 us -> 3.87 us  [body(): correction = (search.astype(jnp.float32) - projection).astype(jnp.bfloat16)]
  transfers between devices with their start and end apart: 4 -> 4, of which waited for: 2 -> 2; matrix products, arithmetic and copies ran while one was open for 7% -> 6% of each run, Pallas kernels for 0% -> 0%
where the time goes in v1:
time: 639 us; the launch traced here: 630 us
  local copies, waits for them, and re-layouts  209 us (33%)
  blocking collectives  152 us (24%)
  matrix products  136 us (21%)
  waiting for transfers between devices  76.7 us (12%)
  other arithmetic  29.6 us (5%)
  starting transfers between devices  23.3 us (4%)
    psum x1, blocking collectives, body(): intersections = lax.psum(intersections, ('band', 'pw')).astype(jnp.bfloat16)  97.9 us
    unnamed x45, local copies, waits for them, and re-layouts  57.7 us
    psum x1, blocking collectives, body(): lax.psum((numerator, denominator, force_part), ('band', 'pw'))  54.3 us
    reshape x3, local copies, waits for them, and re-layouts, body(): applied = jnp.concatenate(received, axis=0)  46.9 us
    dot_general x1, matrix products, section_x(): jnp.einsum('bxycz,cxdn->bnydz', split_up, table_x, preferred_element_type...  43.8 us
    all_to_all x1, waiting for transfers between devices, body(): received = lax.all_to_all(jnp.stack(pieces), ('band', 'pw'), 0, 0)  41.7 us
    all_to_all x1, waiting for transfers between devices, body(): lax.all_to_all(orbitals, ('band', 'pw'), split_axis=0, concat_axis=1, til...  35 us
    dot_general x1, local copies, waits for them, and re-layouts, section_zy_inverse(): jnp.einsum('blydn,dnck->blyck', along_y, table_z, preferred_element_type=...  28.5 us
  transfers between devices with their start and end apart: 4, of which 2 were waited for; matrix products, arithmetic and copies ran while one was open for 6% of the time, Pallas kernels for 0%

profile of v1, /device:TPU:0, one launch (start us, length us, event | category | flops | bytes accessed | tf_op | source)
XLA Modules:
  0.0 630.4 jit_solution(16365451656591374133)
XLA Ops:
  0.6 12.1 %copy.130 = bf16[128,8,2,2048]{3,1,2,0:T(8,128)(2,1)} copy(bf16[128,8,2,2048]{3,2,1,0:T(2,128)(2,1)} %bitcast.257) | data formatting | bytes 16777216
  12.7 5.8 convolution_convert_fusion
  18.5 2.8 reshape.683
  21.3 8.8 %all-to-all-start = ((bf16[256,2,2048]{2,1,0:T(2,128)(2,1)}), bf16[256,2,2048]{2,1,0:T(2,128)(2,1)}, u32[]{:S(2)}, u32[]{:S(2)}) async-start(bf16[256,2,2048]{2,1,0:T(2,128)(2,1)} %reshape.683), calls=%async_computation | async-start | bytes 4194304 | tf_op jit(solution)/shard_map/all_to_all | solution.py:189
  30.7 7.5 %fusion.29 = f32[64,64,64]{2,0,1:T(8,128)} fusion(f32[256,64]{0,1:T(8,128)S(1)} %get-tuple-element.67, f32[256,64]{0,1:T(8,128)S(1)} %get-tuple-element.74, s32[256]{0:T(256)S(1)} %bitcast.266, f32[256]{0:T(256)S(1)} %select_reduce_fusion), kind=kOutput, calls=%fused_computation.35 | convolution fusion | flops 806666240 | bytes 1181696 | tf_op jit(solution)/shard_map/dot_general | solution.py:114
  38.2 35.0 %all-to-all-done = bf16[256,2,2048]{2,1,0:T(2,128)(2,1)} async-done(((bf16[256,2,2048]{2,1,0:T(2,128)(2,1)}), bf16[256,2,2048]{2,1,0:T(2,128)(2,1)}, u32[]{:S(2)}, u32[]{:S(2)}) %all-to-all-start) | async-done | bytes 2097184 | tf_op jit(solution)/shard_map/all_to_all | solution.py:189
  73.2 2.5 copy.91
  77.2 17.9 %reshape.684 = bf16[16,32,32,2,32]{4,3,2,0,1:T(2,128)(2,1)} reshape(bf16[16,16,2,2048]{3,0,2,1:T(8,128)(2,1)} %copy.92) | data formatting | bytes 4194304 | tf_op jit(solution)/shard_map/reshape | solution.py:56
  95.0 12.6 %fusion.20 = bf16[16,32,64,2,64]{4,2,1,0,3:T(8,128)(2,1)} fusion(bf16[16,32,32,2,32,1]{4,3,2,0,1,5:T(2,128)(2,1)} %bitcast.253, bf16[1,32,2,64]{3,1,0,2:T(8,128)(2,1)S(1)} %get-tuple-element.57, bf16[1,32,2,64]{3,1,0,2:T(8,128)(2,1)S(1)} %get-tuple-element.56), kind=kOutput, calls=%fused_computation.24 | convolution fusion | flops 811663360 | bytes 10502144 | tf_op jit(solution)/shard_map/blycz,cydm->blmdz/dot_general | solution.py:60
  107.7 43.8 %fusion.1 = (f32[64,64,64]{2,0,1:T(8,128)}, bf16[16,64,64,2,64]{4,1,2,0,3:T(8,128)(2,1)}) fusion(f32[64,64,64]{2,0,1:T(8,128)} %fusion.29, bf16[16,32,64,2,64]{4,2,1,0,3:T(8,128)(2,1)} %fusion.20, bf16[1,32,2,64]{3,1,0,2:T(8,128)(2,1)S(1)} %get-tuple-element.57, bf16[1,32,2,64]{3,1,0,2:T(8,128)(2,1)S(1)} %get-tuple-element.56), kind=kOutput, calls=%fused_computation.3 | convolution fusion | flops 1107066880 | bytes 27279360 | tf_op jit(solution)/shard_map/bxycz,cxdn->bnydz/dot_general | solution.py:70
  151.5 19.0 %fusion.6 = bf16[16,32,64,2,64,1]{4,1,2,0,3,5:T(8,128)(2,1)} fusion(bf16[16,64,64,2,64]{4,1,2,0,3:T(8,128)(2,1)} %get-tuple-element.40, bf16[1,64,2,32]{1,3,0,2:T(8,128)(2,1)S(1)} %get-tuple-element.55, bf16[1,64,2,32]{1,3,0,2:T(8,128)(2,1)S(1)} %get-tuple-element.54), kind=kOutput, calls=%fused_computation.10 | convolution fusion | flops 1077968896 | bytes 25182208 | tf_op jit(solution)/shard_map/bnydz,dncx->bxycz/dot_general | solution.py:76
  170.5 19.3 %convolution_bitcast_fusion = f32[16,32,32,2,32]{4,2,3,1,0:T(8,128)} fusion(bf16[16,32,64,2,64,1]{4,1,2,0,3,5:T(8,128)(2,1)} %fusion.6, bf16[1,64,2,32]{1,3,0,2:T(8,128)(2,1)S(1)} %get-tuple-element.55, bf16[1,64,2,32]{1,3,0,2:T(8,128)(2,1)S(1)} %get-tuple-element.54), kind=kOutput, calls=%fused_computation.25 | convolution fusion | flops 807469056 | bytes 12599296 | tf_op jit(solution)/shard_map/blydn,dnck->blyck/dot_general | solution.py:89
  189.7 28.5 %copy.97 = f32[16,32,32,2,32]{4,3,2,1,0:T(2,128)} copy(f32[16,32,32,2,32]{4,2,3,1,0:T(8,128)} %convolution_bitcast_fusion) | data formatting | bytes 8388608 | tf_op jit(solution)/shard_map/blydn,dnck->blyck/dot_general | solution.py:89
  218.2 21.7 %reshape.686 = f32[16,32,2048]{2,1,0:T(8,128)} reshape(f32[16,32,32,2,32]{4,3,2,1,0:T(2,128)} %copy.97) | data formatting | bytes 8388608 | tf_op jit(solution)/shard_map/reshape | solution.py:90
  241.9 2.1 fusion.64
  244.0 2.1 fusion.63
  246.1 2.1 fusion.62
  254.3 2.1 fusion.58
  258.4 2.1 fusion.56
  260.5 2.1 fusion.55
  266.7 2.1 fusion.52
  270.8 2.1 fusion.50
  272.9 10.1 %all-to-all-start.1 = ((f32[16,16,2,2048]{3,2,1,0:T(2,128)}), f32[16,16,2,2048]{3,2,1,0:T(2,128)}, u32[]{:S(2)}, u32[]{:S(2)}) async-start(f32[16,16,2,2048]{3,2,1,0:T(2,128)} %fusion.50), calls=%async_computation.1 | async-start | bytes 8388608 | tf_op jit(solution)/shard_map/all_to_all | solution.py:196
  284.4 3.0 collective-permute-start.1
  287.8 5.1 broadcast_multiply_fusion.2
  293.0 3.0 copy.128
  301.0 2.5 copy.106
  303.6 3.4 div.129
  306.9 12.6 %fusion.14 = f32[64,768]{1,0:T(8,128)S(1)} fusion(f32[64,4096]{1,0:T(8,128)} %div.129, f32[256,4096]{0,1:T(8,128)} %bitcast.261, f32[256,4096]{0,1:T(8,128)} %bitcast.262, f32[256,4096]{0,1:T(8,128)} %bitcast.260), kind=kOutput, calls=%fused_computation.18 | convolution fusion | flops 2422210560 | bytes 13828096 | tf_op jit(solution)/shard_map/dot_general | solution.py:124
  319.7 41.7 %all-to-all-done.1 = f32[16,16,2,2048]{3,2,1,0:T(2,128)} async-done(((f32[16,16,2,2048]{3,2,1,0:T(2,128)}), f32[16,16,2,2048]{3,2,1,0:T(2,128)}, u32[]{:S(2)}, u32[]{:S(2)}) %all-to-all-start.1) | async-done | bytes 4194336 | tf_op jit(solution)/shard_map/all_to_all | solution.py:196
  361.4 8.0 %copy.132 = f32[32,8,2,2048]{3,1,2,0:T(8,128)} copy(f32[32,8,2,2048]{3,2,1,0:T(2,128)} %bitcast.101) | data formatting | bytes 8388608
  369.3 18.8 %reshape.709 = f32[256,2,32,2,32]{4,3,2,1,0:T(2,128)} reshape(f32[16,16,2,2048]{3,2,1,0:T(2,128)} %all-to-all-done.1) | data formatting | bytes 8388608 | tf_op jit(solution)/shard_map/reshape | solution.py:197
  388.1 20.8 %copy.102 = f32[256,2,32,2,32]{0,4,3,2,1:T(8,128)} copy(f32[256,2,32,2,32]{4,3,2,1,0:T(2,128)} %reshape.709) | data formatting | bytes 8388608 | tf_op jit(solution)/shard_map/reshape | solution.py:197
  408.9 3.3 fusion.32
  412.2 54.3 %all-reduce.1 = (f32[256]{0:T(256)S(1)}, f32[256]{0:T(256)S(1)}) all-reduce(f32[256]{0:T(256)S(1)} %get-tuple-element.25, f32[256]{0:T(256)S(1)} %get-tuple-element.24), channel_id=1, replica_groups=mesh['img'=2,'band'=4,'pw'=4] {'band','pw'}, use_global_device_ids=true, to_apply=%region_4.5 | all-reduce | flops 512 | bytes 4096 | tf_op jit(solution)/shard_map/psum | solution.py:204
  466.5 4.7 fusion.36
  473.9 2.9 copy.103
  476.7 8.2 %multiply_bitcast_fusion = f32[1024,512]{0,1:T(8,128)S(1)} fusion(bf16[1024,4096]{1,0:T(8,128)(2,1)} %bitcast.247, bf16[256,4096]{1,0:T(8,128)(2,1)} %copy.103, bf16[256,4096]{1,0:T(8,128)(2,1)} %fusion.36), kind=kOutput, calls=%fused_computation.54 | convolution fusion | flops 4303880192 | bytes 14680064 | tf_op jit(solution)/shard_map/ik,jk->ij/dot_general | solution.py:215
  485.0 97.9 %all-reduce.3 = (bf16[1024,512]{0,1:T(8,128)(2,1)}, f32[3,256]{1,0:T(4,128)S(1)}) all-reduce(f32[1024,512]{0,1:T(8,128)S(1)} %multiply_bitcast_fusion, f32[3,256]{1,0:T(4,128)S(1)} %pad_maximum_fusion.9), channel_id=1, replica_groups=mesh['img'=2,'band'=4,'pw'=4] {'band','pw'}, use_global_device_ids=true, to_apply=%region_5.6 | all-reduce | flops 525056 | bytes 3151872 | tf_op jit(solution)/shard_map/psum | solution.py:218
  584.8 7.2 %fusion.163 = f32[512,4096]{1,0:T(8,128)S(1)} fusion(bf16[1024,512]{0,1:T(8,128)(2,1)} %get-tuple-element.29, bf16[1024,4096]{1,0:T(8,128)(2,1)} %bitcast.248), kind=kOutput, calls=%fused_computation.244 | convolution fusion | flops 4294967296 | bytes 17825792 | tf_op jit(solution)/shard_map/ij,ik->jk/dot_general | solution.py:219
  592.0 3.7 fusion.157
  595.7 5.6 copy.104
  601.3 4.1 slice_negate_fusion
  605.4 5.6 copy.127
  611.0 7.2 %copy.98 = f32[1,256,2,2048]{1,3,2,0:T(8,128)} copy(f32[1,256,2,2048]{3,2,1,0:T(2,128)} %bitcast.62) | data formatting | bytes 8388608 | tf_op jit(solution)/shard_map/reshape | solution.py:197
  618.3 2.1 pad_maximum_fusion
  622.4 3.9 subtract_convert_fusion
  626.3 3.9 copy.107
  (67 shorter events, 29.0 us)
Async XLA Ops:
  0.6 12.1 %copy-start = (bf16[1,1024,256]{2,1,0:T(8,128)(2,1)S(1)}, bf16[1,1024,256]{2,1,0:T(8,128)(2,1)}, u32[]{:S(2)}) copy-start(bf16[1,1024,256]{2,1,0:T(8,128)(2,1)} %param.8) | copy-start | bytes 1572868
  18.5 12.0 %copy-start.10 = (s32[256]{0:T(256)S(1)}, s32[256]{0:T(256)}, u32[]{:S(2)}) copy-start(s32[256]{0:T(256)} %param.12) | copy-start | bytes 3076
  18.5 12.0 %copy-start.11 = (f32[4]{0:T(128)S(1)}, f32[4]{0:T(128)}, u32[]{:S(2)}) copy-start(f32[4]{0:T(128)} %param.13) | copy-start | bytes 52
  18.5 12.1 %copy-start.6 = (s32[1,3,256]{2,0,1:T(1,128)S(1)}, s32[1,3,256]{2,0,1:T(1,128)}, u32[]{:S(2)}) copy-start(s32[1,3,256]{2,0,1:T(1,128)} %param.9) | copy-start | bytes 9220
  21.3 51.8 %all-to-all-start = ((bf16[256,2,2048]{2,1,0:T(2,128)(2,1)}), bf16[256,2,2048]{2,1,0:T(2,128)(2,1)}, u32[]{:S(2)}, u32[]{:S(2)}) async-start(bf16[256,2,2048]{2,1,0:T(2,128)(2,1)} %reshape.683), calls=%async_computation | async-start | bytes 4194304 | tf_op jit(solution)/shard_map/all_to_all | solution.py:189
  272.9 88.4 %all-to-all-start.1 = ((f32[16,16,2,2048]{3,2,1,0:T(2,128)}), f32[16,16,2,2048]{3,2,1,0:T(2,128)}, u32[]{:S(2)}, u32[]{:S(2)}) async-start(f32[16,16,2,2048]{3,2,1,0:T(2,128)} %fusion.50), calls=%async_computation.1 | async-start | bytes 8388608 | tf_op jit(solution)/shard_map/all_to_all | solution.py:196
  283.1 12.9 %collective-permute-start = (s32[3,256]{1,0:T(4,128)S(1)}, s32[3,256]{1,0:T(4,128)S(1)}, u32[]{:S(2)}, u32[]{:S(2)}) collective-permute-start(s32[3,256]{1,0:T(4,128)S(1)} %bitcast.273), channel_id=1, source_target_pairs={{16,0},{17,1},{18,2},{19,3},{20,4},{21,5},{22,6},{23,7},{24,8},{25... | collective-permute-start | bytes 9224 | tf_op jit(solution)/shard_map/ppermute | solution.py:22
  284.4 11.6 %collective-permute-start.1 = (s32[3,256]{1,0:T(4,128)S(1)}, s32[3,256]{1,0:T(4,128)S(1)}, u32[]{:S(2)}, u32[]{:S(2)}) collective-permute-start(s32[3,256]{1,0:T(4,128)S(1)} %bitcast.274), channel_id=1, source_target_pairs={{0,16},{1,17},{2,18},{3,19},{4,20},{5,21},{6,22},{7,23},{8,24},{9,... | collective-permute-start | bytes 9224 | tf_op jit(solution)/shard_map/ppermute | solution.py:22
  292.9 3.1 copy-start.8
  292.9 3.1 copy-start.9
  466.5 153.9 %copy-start.7 = (f32[256]{0:T(256)}, f32[256]{0:T(256)S(1)}, u32[]{:S(2)}) copy-start(f32[256]{0:T(256)S(1)} %add_divide_fusion) | copy-start | bytes 3076
  466.5 4.7 copy-start.2
  466.5 5.5 copy-start.4
  618.3 2.8 copy-start.3
  618.3 4.1 copy-start.5
  622.4 7.8 %copy-start.1 = (bf16[1,1024,256]{2,1,0:T(8,128)(2,1)S(1)}, bf16[1,1024,256]{2,1,0:T(8,128)(2,1)}, u32[]{:S(2)}) copy-start(bf16[1,1024,256]{2,1,0:T(8,128)(2,1)} %param.8) | copy-start | bytes 1572868
